TPU v7x, 256 devices: a whole 4x4x8 slice. The times are simulated.
256 devices in a mesh: chan: 2 (over x_lo), elem: 8 (over y, x_hi), beam: 16 (over z, core).
Axes of the slice: x: 4 (x_hi: 2, x_lo: 2; x = x_hi * 2 + x_lo), y: 4, z: 8, core: 2. Of those that a mesh axis runs over, the one named last changes fastest.
Arguments:
- voltages: bfloat16 [2, 128, 256, 2048], P(None, 'chan', 'beam', 'elem'), may hold values from -6 to 6
- weights: bfloat16 [2, 128, 2048, 2048], P(None, 'chan', 'elem', 'beam'), may hold values from -0.09375 to 0.09375
Outputs:
- power: float32 [128, 256, 2048], P(None, ('chan', 'elem'), 'beam')
All inputs are finite; a program needn't handle non-finite values.
Results may differ from a plain program's by a relative error of at most 0.012.
Values may be sent and summed in bfloat16 or wider, within the bound.
A program may use at most 128 MiB of HBM per device.

v0:
```python
import jax
import jax.numpy as jnp
from jax import lax
from jax.sharding import PartitionSpec as P


def dft_tables(channels):
    index = jnp.arange(channels, dtype=jnp.int32)
    phase = index[:, None] * index[None, :] % channels
    angle = phase.astype(jnp.float32) * (2.0 * jnp.pi / channels)
    factor = 1.0 / jnp.sqrt(jnp.float32(channels))
    return (jnp.cos(angle) * factor, jnp.sin(angle) * factor)


def shards(voltages, weights):
    local_beams = weights.shape[3]
    volt_piece = lax.all_gather(voltages, "beam", axis=2, tiled=True)
    real_part = jnp.einsum(
        "cte,ceb->ctb", volt_piece[0], weights[0], preferred_element_type=jnp.float32
    ) - jnp.einsum("cte,ceb->ctb", volt_piece[1], weights[1], preferred_element_type=jnp.float32)
    imag_part = jnp.einsum(
        "cte,ceb->ctb", volt_piece[0], weights[1], preferred_element_type=jnp.float32
    ) + jnp.einsum("cte,ceb->ctb", volt_piece[1], weights[0], preferred_element_type=jnp.float32)
    partial_value = jnp.stack([real_part, imag_part])
    summed = lax.psum_scatter(
        partial_value.astype(jnp.bfloat16), "elem", scatter_dimension=1, tiled=True
    )
    owned = lax.all_to_all(summed, ("chan", "elem"), split_axis=2, concat_axis=1, tiled=True)
    channels = owned.shape[1]
    own_time = owned.shape[2]
    cosine, sine = dft_tables(channels)
    real_in = owned[0].astype(jnp.float32).reshape(channels, own_time * local_beams)
    imag_in = owned[1].astype(jnp.float32).reshape(channels, own_time * local_beams)
    highest = lax.Precision.HIGHEST
    real_out = jnp.dot(
        cosine, real_in, precision=highest, preferred_element_type=jnp.float32
    ) - jnp.dot(sine, imag_in, precision=highest, preferred_element_type=jnp.float32)
    imag_out = jnp.dot(
        sine, real_in, precision=highest, preferred_element_type=jnp.float32
    ) + jnp.dot(cosine, imag_in, precision=highest, preferred_element_type=jnp.float32)
    power = real_out * real_out + imag_out * imag_out
    return power.reshape(channels, own_time, local_beams)


def solution(mesh):
    placed = (P(None, "chan", "beam", "elem"), P(None, "chan", "elem", "beam"))
    return jax.shard_map(
        shards,
        mesh=mesh,
        in_specs=placed,
        out_specs=P(None, ("chan", "elem"), "beam"),
        check_vma=False,
    )
```

profile of v0, /device:TPU:32, one launch (start us, length us, event | category | flops | bytes accessed | tf_op | source)
XLA Modules:
  0.0 328.4 jit_solution(3343616162390138863)
XLA Ops:
  6.5 0.0 all-gather.2.cloned.1.call-start
  6.5 0.7 all-gather.2.cloned.1.call-update
  7.3 0.0 reduce-scatter.5.cloned.1.call-start
  7.3 97.9 %all-gather.2.cloned.1.call-done = bf16[2,64,256,256]{3,2,1,0:T(8,128)(2,1)} async-done(((bf16[2,64,16,256]{3,2,1,0:T(8,128)(2,1)}), bf16[2,64,256,256]{3,2,1,0:T(8,128)(2,1)}) %all-gather.2.cloned.1.call-update) | async-done | bytes 16777232 | tf_op jit(solution)/shard_map/all_gather | solution.py:17
  105.2 10.1 %fusion = f32[64,256,128]{2,1,0:T(8,128)} fusion(bf16[2,64,256,256]{3,2,1,0:T(8,128)(2,1)} %all-gather.2.cloned.1.call-done, bf16[2,64,256,128]{3,2,1,0:T(8,128)(2,1)} %param.3), kind=kOutput, calls=%fused_computation.6 | convolution fusion | flops 1073741824 | bytes 20971520 | tf_op jit(solution)/shard_map/cte,ceb->ctb/dot_general | solution.py:21
  115.4 10.1 %fusion.1 = f32[64,256,128]{2,1,0:T(8,128)} fusion(bf16[2,64,256,256]{3,2,1,0:T(8,128)(2,1)} %all-gather.2.cloned.1.call-done, bf16[2,64,256,128]{3,2,1,0:T(8,128)(2,1)} %param.3), kind=kOutput, calls=%fused_computation.7 | convolution fusion | flops 1073741824 | bytes 20971520 | tf_op jit(solution)/shard_map/cte,ceb->ctb/dot_general | solution.py:18
  125.5 11.4 %fusion.5 = bf16[1,64,256,128]{3,2,1,0:T(8,128)(2,1)} fusion(f32[64,256,128]{2,1,0:T(8,128)} %fusion, bf16[2,64,256,128]{3,2,1,0:T(8,128)(2,1)} %param.3, bf16[2,64,256,256]{3,2,1,0:T(8,128)(2,1)} %all-gather.2.cloned.1.call-done), kind=kOutput, calls=%fused_computation.11 | convolution fusion | flops 1077936128 | bytes 25165824 | tf_op jit(solution)/shard_map/cte,ceb->ctb/dot_general | solution.py:23
  136.9 11.3 %fusion.4 = bf16[1,64,256,128]{3,2,1,0:T(8,128)(2,1)} fusion(f32[64,256,128]{2,1,0:T(8,128)} %fusion.1, bf16[2,64,256,128]{3,2,1,0:T(8,128)(2,1)} %param.3, bf16[2,64,256,256]{3,2,1,0:T(8,128)(2,1)} %all-gather.2.cloned.1.call-done), kind=kOutput, calls=%fused_computation.10 | convolution fusion | flops 1077936128 | bytes 25165824 | tf_op jit(solution)/shard_map/cte,ceb->ctb/dot_general | solution.py:20
  148.2 7.4 %pad_maximum_fusion = bf16[2,64,256,128]{3,2,1,0:T(8,128)(2,1)} fusion(bf16[1,64,256,128]{3,2,1,0:T(8,128)(2,1)} %fusion.5, bf16[1,64,256,128]{3,2,1,0:T(8,128)(2,1)} %fusion.4), kind=kLoop, calls=%fused_computation.3 | loop fusion | flops 4194304 | bytes 16777216 | tf_op jit(solution)/shard_map/stack | solution.py:24
  155.7 7.7 %copy.6 = bf16[2,64,256,128]{3,2,0,1:T(8,128)(2,1)} copy(bf16[2,64,256,128]{3,2,1,0:T(8,128)(2,1)} %pad_maximum_fusion) | data formatting | bytes 16777216
  163.4 12.2 %copy.33 = bf16[8,8,512,128]{3,1,2,0:T(8,128)(2,1)} copy(bf16[8,8,512,128]{3,2,1,0:T(8,128)(2,1)} %bitcast.69) | data formatting | bytes 16777216
  175.6 0.0 reduce-scatter.5.cloned.1.call-update
  175.6 120.1 %reduce-scatter.5.cloned.1.call-done = bf16[8,65536]{1,0:T(8,128)(2,1)} async-done(((bf16[64,65536]{1,0:T(8,128)(2,1)}), bf16[8,65536]{1,0:T(8,128)(2,1)}) %reduce-scatter.5.cloned.1.call-update) | async-done | bytes 1048592
  295.7 1.4 copy.4
  297.1 19.2 %all_to_all.15 = bf16[2,8,256,128]{3,1,0,2:T(8,128)(2,1)S(1)} all-to-all(bf16[2,8,256,128]{3,1,0,2:T(8,128)(2,1)S(1)} %copy.4), channel_id=1, replica_groups=mesh['chan'=2,'elem'=8,'beam'=16] {'chan','elem'}, dimensions={2} | all-to-all | bytes 2097152 | tf_op jit(solution)/shard_map/all_to_all | solution.py:28
  316.4 0.3 copy.34
  316.7 0.3 slice_bitcast_fusion.10
  316.9 0.8 fusion.24
  317.8 0.8 fusion.26
  318.6 0.8 fusion.16
  319.5 0.9 fusion.21
  320.4 1.2 copy.13
Async XLA Ops:
  6.5 98.7 %all-gather.2.cloned.1.call-start = ((), (), s32[]{:S(2)}) async-start(), calls=%async_computation.2 | async-start | bytes 17825792 | tf_op jit(solution)/shard_map/all_gather | solution.py:17
  7.3 288.5 %reduce-scatter.5.cloned.1.call-start = ((), (), s32[]{:S(2)}) async-start(), calls=%async_computation.3 | async-start | bytes 9437184
Sparse Core Ops, SparseCore 0:
  9.2 96.0 all-gather.1
  175.7 119.9 reduce-scatter.4
where the time goes:
time: 329 us; the launch traced here: 328 us
  waiting for transfers between devices  219 us (67%)
  matrix products  46.4 us (14%)
  local copies, waits for them, and re-layouts  23 us (7%)
  blocking collectives  19.2 us (6%)
  between operations  13.4 us (4%)
  other arithmetic  7.45 us (2%)
    unnamed x3, waiting for transfers between devices  121 us
    all_gather x1, waiting for transfers between devices, shards(): volt_piece = lax.all_gather(voltages, 'beam', axis=2, tiled=True)  97.9 us
    unnamed x4, local copies, waits for them, and re-layouts  21.3 us
    all_to_all x1, blocking collectives, shards(): lax.all_to_all(summed, ('chan', 'elem'), split_axis=2, concat_axis=1, til...  19.2 us
    dot_general x1, matrix products, shards(): jnp.einsum('cte,ceb->ctb', volt_piece[1], weights[0], preferred_element_t...  11.4 us
    dot_general x1, matrix products, shards(): jnp.einsum('cte,ceb->ctb', volt_piece[1], weights[1], preferred_element_t...  11.3 us
    dot_general x1, matrix products, shards(): jnp.einsum('cte,ceb->ctb', volt_piece[0], weights[0], preferred_element_t...  10.1 us
    dot_general x1, matrix products, shards(): jnp.einsum('cte,ceb->ctb', volt_piece[0], weights[1], preferred_element_t...  10.1 us
  transfers between devices with their start and end apart: 2, of which 2 were waited for; matrix products, arithmetic and copies ran while one was open for 0% of the time, Pallas kernels for 0%

commit v1 on v0

--- a/solution.py
+++ b/solution.py
@@ -14,7 +14,10 @@
 
 def shards(voltages, weights):
     local_beams = weights.shape[3]
-    volt_piece = lax.all_gather(voltages, "beam", axis=2, tiled=True)
+    size = lax.axis_size("beam")
+    tiles = jnp.stack([voltages for _ in range(size)])
+    tiles = lax.all_to_all(tiles, "beam", split_axis=0, concat_axis=0)
+    volt_piece = jnp.concatenate(tiles, axis=2)
     real_part = jnp.einsum(
         "cte,ceb->ctb", volt_piece[0], weights[0], preferred_element_type=jnp.float32
     ) - jnp.einsum("cte,ceb->ctb", volt_piece[1], weights[1], preferred_element_type=jnp.float32)

time: 329 us -> 618 us (1.88)
  blocking collectives: 19.2 us -> 390 us
  waiting for transfers between devices: 219 us -> 120 us
  local copies, waits for them, and re-layouts: 23 us -> 48.5 us
  matrix products: 46.4 us -> 39.9 us
    all_to_all x0 -> x1, blocking collectives: none -> 371 us  [shards(): tiles = lax.all_to_all(tiles, 'beam', split_axis=0, concat_axis=0)]
    all_gather x1 -> x0, waiting for transfers between devices: 97.9 us -> none  [shards(): volt_piece = lax.all_gather(voltages, 'beam', axis=2, tiled=True)]
    slice x0 -> x3, local copies, waits for them, and re-layouts: none -> 21.8 us  [the longest x2 13.8 us: shards(): volt_piece[1]]
    unnamed x3 -> x2, waiting for transfers between devices: 121 us -> 120 us
    unnamed x4 -> x10, local copies, waits for them, and re-layouts: 21.3 us -> 21.4 us
  transfers between devices with their start and end apart: 2 -> 1, of which waited for: 2 -> 1; matrix products, arithmetic and copies ran while one was open for 0% -> 0% of each run, Pallas kernels for 0% -> 0%
where the time goes in v1:
time: 618 us
  blocking collectives  390 us (63%)
  waiting for transfers between devices  120 us (19%)
  local copies, waits for them, and re-layouts  48.5 us (8%)
  matrix products  39.9 us (6%)
  between operations  13.5 us (2%)
  other arithmetic  6.19 us (1%)
    all_to_all x1, blocking collectives, shards(): tiles = lax.all_to_all(tiles, 'beam', split_axis=0, concat_axis=0)  371 us
    unnamed x2, waiting for transfers between devices  120 us
    unnamed x10, local copies, waits for them, and re-layouts  21.4 us
    all_to_all x1, blocking collectives, shards(): lax.all_to_all(summed, ('chan', 'elem'), split_axis=2, concat_axis=1, til...  19.3 us
    slice x2, local copies, waits for them, and re-layouts, shards(): volt_piece[1]  13.8 us
  transfers between devices with their start and end apart: 1, of which 1 were waited for; matrix products, arithmetic and copies ran while one was open for 0% of the time, Pallas kernels for 0%

profile of v1, /device:TPU:32, one launch (start us, length us, event | category | flops | bytes accessed | tf_op | source)
XLA Modules:
  0.0 617.9 jit_solution(3502128271423559940)
XLA Ops:
  6.5 3.6 stack.11
  10.2 370.9 %all_to_all.20 = bf16[16,2,64,16,256]{4,3,2,1,0:T(8,128)(2,1)S(1)} all-to-all(bf16[16,2,64,16,256]{4,3,2,1,0:T(8,128)(2,1)S(1)} %stack.11), channel_id=1, replica_groups=mesh['chan'=2,'elem'=8,'beam'=16] {'beam'}, dimensions={0} | all-to-all | bytes 33554432 | tf_op jit(solution)/shard_map/all_to_all | solution.py:19
  381.1 6.0 fusion.66
  387.1 7.9 %copy.5 = bf16[1,64,16,16,256]{4,3,2,1,0:T(8,128)(2,1)} copy(bf16[1,64,16,16,256]{4,3,1,0,2:T(8,128)(2,1)} %get-tuple-element.5) | data formatting | bytes 16777216 | tf_op jit(solution)/shard_map/slice | solution.py:23
  394.9 8.0 %copy.4 = bf16[1,64,16,16,256]{4,3,2,1,0:T(8,128)(2,1)} copy(bf16[1,64,16,16,256]{4,3,1,0,2:T(8,128)(2,1)} %get-tuple-element.6) | data formatting | bytes 16777216 | tf_op jit(solution)/shard_map/slice | solution.py:22
  402.9 10.3 %fusion.4 = f32[64,256,128]{2,1,0:T(8,128)} fusion(bf16[64,256,256]{2,1,0:T(8,128)(2,1)} %bitcast.63, bf16[2,64,256,128]{3,2,1,0:T(8,128)(2,1)} %param.3), kind=kOutput, calls=%fused_computation.8 | convolution fusion | flops 1073741824 | bytes 20971520 | tf_op jit(solution)/shard_map/cte,ceb->ctb/dot_general | solution.py:23
  413.2 0.0 copy-done
  413.2 5.6 fusion.2
  418.8 9.4 %fusion = bf16[1,64,256,128]{3,2,1,0:T(8,128)(2,1)S(1)} fusion(f32[64,256,128]{2,1,0:T(8,128)} %fusion.4, bf16[64,256,256]{2,1,0:T(8,128)(2,1)} %bitcast.65, bf16[2,64,256,128]{3,2,1,0:T(8,128)(2,1)} %param.3), kind=kOutput, calls=%fused_computation.4 | convolution fusion | flops 1077936128 | bytes 25165824 | tf_op jit(solution)/shard_map/cte,ceb->ctb/dot_general | solution.py:21
  428.2 11.3 %fusion.1 = bf16[1,64,256,128]{3,2,1,0:T(8,128)(2,1)} fusion(f32[64,256,128]{2,1,0:T(8,128)} %fusion.2, bf16[64,256,256]{2,1,0:T(8,128)(2,1)} %bitcast.64, bf16[2,64,256,128]{3,2,1,0:T(8,128)(2,1)} %param.3), kind=kOutput, calls=%fused_computation.5 | convolution fusion | flops 1077936128 | bytes 25165824 | tf_op jit(solution)/shard_map/cte,ceb->ctb/dot_general | solution.py:26
  439.5 6.2 %pad_maximum_fusion = bf16[2,64,256,128]{3,2,1,0:T(8,128)(2,1)} fusion(bf16[1,64,256,128]{3,2,1,0:T(8,128)(2,1)} %fusion.1, bf16[1,64,256,128]{3,2,1,0:T(8,128)(2,1)S(1)} %fusion), kind=kLoop, calls=%fused_computation.1 | loop fusion | flops 4194304 | bytes 16777216 | tf_op jit(solution)/shard_map/stack | solution.py:27
  445.7 7.9 %copy.8 = bf16[2,64,256,128]{3,2,0,1:T(8,128)(2,1)} copy(bf16[2,64,256,128]{3,2,1,0:T(8,128)(2,1)} %pad_maximum_fusion) | data formatting | bytes 16777216
  453.6 12.0 %copy.35 = bf16[8,8,512,128]{3,1,2,0:T(8,128)(2,1)} copy(bf16[8,8,512,128]{3,2,1,0:T(8,128)(2,1)} %bitcast.71) | data formatting | bytes 16777216
  465.6 0.0 reduce-scatter.5.cloned.1.call-update
  465.6 119.6 %reduce-scatter.5.cloned.1.call-done = bf16[8,65536]{1,0:T(8,128)(2,1)} async-done(((bf16[64,65536]{1,0:T(8,128)(2,1)}), bf16[8,65536]{1,0:T(8,128)(2,1)}) %reduce-scatter.5.cloned.1.call-update) | async-done | bytes 1048592
  585.2 1.4 copy.6
  586.6 19.3 %all_to_all.21 = bf16[2,8,256,128]{3,1,0,2:T(8,128)(2,1)S(1)} all-to-all(bf16[2,8,256,128]{3,1,0,2:T(8,128)(2,1)S(1)} %copy.6), channel_id=1, replica_groups=mesh['chan'=2,'elem'=8,'beam'=16] {'chan','elem'}, dimensions={2} | all-to-all | bytes 2097152 | tf_op jit(solution)/shard_map/all_to_all | solution.py:31
  605.9 0.3 copy.36
  606.1 0.3 slice_bitcast_fusion
  606.4 0.8 fusion.24
  607.3 0.8 fusion.26
  608.1 0.8 fusion.20
  609.0 0.9 fusion.21
  609.9 1.2 copy.15
  (7 shorter events, 0.0 us)
Async XLA Ops:
  6.5 578.7 %reduce-scatter.5.cloned.1.call-start = ((), (), s32[]{:S(2)}) async-start(), calls=%async_computation.3 | async-start | bytes 9437184
  394.9 18.3 %slice-start = ((s8[8388608]{0:T(1024)(128)(4,1)}), s8[4194304]{0:T(1024)(128)(4,1)S(1)}, s32[]{:S(2)}) async-start(s8[8388608]{0:T(1024)(128)(4,1)} %bitcast.68), calls=%async_computation.4 | async-start | bytes 8388608
  402.9 10.3 %copy-start = (bf16[1,64,16,16,256]{4,3,2,1,0:T(8,128)(2,1)S(1)}, bf16[1,64,16,16,256]{4,3,2,1,0:T(8,128)(2,1)}, u32[]{:S(2)}) copy-start(bf16[1,64,16,16,256]{4,3,2,1,0:T(8,128)(2,1)} %copy.4) | copy-start | bytes 25165828
  402.9 10.3 %slice-start.1 = ((s8[8388608]{0:T(1024)(128)(4,1)}), s8[4194304]{0:T(1024)(128)(4,1)S(1)}, s32[]{:S(2)}) async-start(s8[8388608]{0:T(1024)(128)(4,1)} %bitcast.68), calls=%async_computation.5 | async-start | bytes 8388608
Sparse Core Ops, SparseCore 0:
  465.7 119.4 reduce-scatter.4
